TPU v7x, 128 devices: a whole 4x4x4 slice. The times are simulated.
128 devices in a mesh: dp: 32 (over y, z, core), tensor: 4 (over x).
Axes of the slice: x: 4, y: 4, z: 4, core: 2. Of those that a mesh axis runs over, the one named last changes fastest.
Arguments:
- tokens: bfloat16 [16384, 4096], P('dp', 'tensor'), may hold values from -6 to 6
- grad_out: bfloat16 [16384, 4096], P('dp'), may hold values from -3 to 3
- gate_pre: bfloat16 [16384, 14336], P('dp', 'tensor'), may hold values from -9 to 9
- up_value: bfloat16 [16384, 14336], P('dp', 'tensor'), may hold values from -6 to 6
- down_weight: bfloat16 [14336, 4096], P('tensor', 'dp'), may hold values from -0.09375 to 0.09375
- in_proj: bfloat16 [128, 4096], P(None, 'tensor'), may hold values from -0.09375 to 0.09375
- out_proj: bfloat16 [128, 14336], P(None, 'tensor'), may hold values from -0.046875 to 0.046875
- test_matrix: bfloat16 [16384, 128], replicated, may hold values from -0.046875 to 0.046875
Outputs:
- factor: float32 [16384, 128], P(('dp', 'tensor'))
All inputs are finite; a program needn't handle non-finite values.
Results may differ from a plain program's by a relative error of at most 0.0065.
The roundings to bfloat16 on the way count: a program that leaves them out, or rounds other values in their place, can miss the bound.
Values may be sent and summed in bfloat16 or wider, within the bound.
A program may use at most 128 MiB of HBM per device.

v0:
```python
import jax
import jax.numpy as jnp
from jax import lax
from jax.sharding import PartitionSpec as P

SEQ_LEN = 128
shift_scale = 0.1
tiny_value = 1e-06


def local(tokens, grad_out, gate_pre, up_value, down_weight, in_proj, out_proj, test_matrix):
    rows = grad_out.shape[0]
    hidden_grad = lax.dot_general(
        grad_out,
        lax.all_gather(down_weight, "dp", axis=1, tiled=True),
        (((1,), (1,)), ((), ())),
        preferred_element_type=jnp.float32,
    )
    gate_wide = gate_pre.astype(jnp.float32)
    logistic = jax.nn.sigmoid(gate_wide)
    gate_grad = (
        hidden_grad * up_value.astype(jnp.float32) * logistic * (1.0 + gate_wide * (1.0 - logistic))
    ).astype(jnp.bfloat16)
    act_part = lax.dot_general(
        tokens, in_proj, (((1,), (1,)), ((), ())), preferred_element_type=jnp.float32
    )
    out_part = lax.dot_general(
        gate_grad, out_proj, (((1,), (1,)), ((), ())), preferred_element_type=jnp.float32
    )
    act_sum, out_sum = lax.psum((act_part, out_part), "tensor")
    pdim = in_proj.shape[0]
    rank_cols = test_matrix.shape[1]
    seqs_here = rows // SEQ_LEN
    act_seq = act_sum.astype(jnp.bfloat16).reshape(seqs_here, SEQ_LEN, pdim)
    out_seq = out_sum.astype(jnp.bfloat16).reshape(seqs_here, SEQ_LEN, pdim)
    proj_grad = (
        jnp.einsum("slp,slq->spq", act_seq, out_seq, preferred_element_type=jnp.float32)
        .astype(jnp.bfloat16)
        .reshape(seqs_here, pdim * pdim)
    )
    coeff = jnp.dot(proj_grad, test_matrix, preferred_element_type=jnp.float32).astype(jnp.bfloat16)
    dp_count = lax.axis_size("dp")
    tp_count = lax.axis_size("tensor")
    tp_index = lax.axis_index("tensor")
    dp_index = lax.axis_index("dp")
    width = pdim * pdim // (dp_count * tp_count)
    picked = lax.dynamic_slice_in_dim(
        proj_grad.reshape(seqs_here, dp_count, tp_count, width), tp_index, 1, 2
    ).reshape(seqs_here, dp_count * width)
    omega_wide = test_matrix.astype(jnp.float32)
    omega_picked = lax.dynamic_slice_in_dim(
        omega_wide.reshape(dp_count, tp_count, width, rank_cols), tp_index, 1, 1
    ).reshape(dp_count * width, rank_cols)
    omega_own = lax.dynamic_slice_in_dim(omega_picked, dp_index * width, width, 0)
    sketch_part = lax.dot_general(
        picked, coeff, (((0,), (0,)), ((), ())), preferred_element_type=jnp.float32
    )
    gram = lax.dot_general(
        test_matrix, test_matrix, (((0,), (0,)), ((), ())), preferred_element_type=jnp.float32
    )
    omega_sq = jnp.trace(gram)
    summed = lax.psum(sketch_part, "dp")
    core_local = lax.dot_general(
        omega_picked, summed, (((0,), (0,)), ((), ())), precision=lax.Precision.HIGHEST
    )
    square_sum, core_sketch = lax.psum((jnp.sum(summed * summed), core_local), "tensor")
    own_rows = lax.dynamic_slice_in_dim(summed, dp_index * width, width, 0)
    shift = shift_scale * jnp.sqrt(square_sum / (omega_sq + tiny_value))
    core = core_sketch + shift * gram
    core = 0.5 * (core + core.T)
    lower = jnp.linalg.cholesky(core)
    shifted = own_rows + shift * omega_own
    factor = jax.scipy.linalg.solve_triangular(lower, shifted.T, lower=True).T
    return factor


def solution(mesh):
    in_specs = (
        P("dp", "tensor"),
        P("dp", None),
        P("dp", "tensor"),
        P("dp", "tensor"),
        P("tensor", "dp"),
        P(None, "tensor"),
        P(None, "tensor"),
        P(),
    )
    out_specs = P(("dp", "tensor"), None)
    return jax.shard_map(local, mesh=mesh, in_specs=in_specs, out_specs=out_specs, check_vma=False)
```

profile of v0, /device:TPU:0, one launch (start us, length us, event | category | flops | bytes accessed | tf_op | source)
XLA Modules:
  0.0 362.2 jit_solution(9847140538251873871)
XLA Ops:
  6.5 0.0 copy-start
  6.5 0.0 all-gather.2.cloned.1.call-start
  6.5 0.7 all-gather.2.cloned.1.call-update
  7.3 0.0 all-reduce.5.cloned.1.call-start
  7.3 0.5 copy-done
  7.8 1.4 fusion.24
  9.1 116.3 %all-gather.2.cloned.1.call-done = bf16[3584,4096]{1,0:T(8,128)(2,1)} async-done(((bf16[3584,128]{1,0:T(8,128)(2,1)}), bf16[3584,4096]{1,0:T(8,128)(2,1)}) %all-gather.2.cloned.1.call-update) | async-done | bytes 29360144 | tf_op jit(solution)/shard_map/all_gather | solution.py:15
  125.4 24.7 %fusion.25 = f32[512,128]{1,0:T(8,128)S(1)} fusion(bf16[128,3584]{1,0:T(8,128)(2,1)} %param.14, bf16[512,3584]{1,0:T(8,128)(2,1)} %param.10, bf16[512,3584]{1,0:T(8,128)(2,1)} %param.11, bf16[512,4096]{1,0:T(8,128)(2,1)} %param.9, bf16[3584,4096]{1,0:T(8,128)(2,1)} %all-gather.2.cloned.1.call-done), kind=kOutput, calls=%fused_computation.40 | convolution fusion | flops 15524167680 | bytes 42074112 | tf_op jit(solution)/shard_map/dot_general | solution.py:27
  150.1 23.1 %all-reduce.8 = (bf16[512,128]{1,0:T(8,128)(2,1)S(1)}, bf16[512,128]{1,0:T(8,128)(2,1)S(1)}) all-reduce(f32[512,128]{1,0:T(8,128)S(1)} %fusion.24, f32[512,128]{1,0:T(8,128)S(1)} %fusion.25), channel_id=1, replica_groups=mesh['dp'=32,'tensor'=4] {'tensor'}, use_global_device_ids=true, to_apply=%region_0.0 | all-reduce | flops 131072 | bytes 786432 | tf_op jit(solution)/shard_map/psum | solution.py:30
  173.2 0.2 convolution_convert_fusion
  173.4 0.2 dynamic-slice_reduce_fusion
  173.6 4.7 %fusion.6 = f32[4096,128]{0,1:T(8,128)} fusion(bf16[16384,128]{1,0:T(8,128)(2,1)} %param.15, bf16[1,4,128,128]{3,2,1,0:T(8,128)(2,1)S(1)} %bitcast.60, bf16[1,4,32,128]{3,2,1,0:T(8,128)(2,1)S(1)} %bitcast.61), kind=kOutput, calls=%fused_computation.12 | convolution fusion | flops 20972032 | bytes 6455296 | tf_op jit(solution)/shard_map/dot_general | solution.py:55
  178.3 0.0 all-reduce.5.cloned.1.call-update
  178.3 0.2 all-reduce.7.cloned.1.call-start
  178.6 5.4 %select_reduce_fusion.1 = (f32[]{:T(128)}, f32[128,128]{1,0:T(8,128)S(1)}) fusion(bf16[16384,128]{1,0:T(8,128)(2,1)} %param.15), kind=kOutput, calls=%fused_computation.29 | convolution fusion | flops 536920064 | bytes 4259844 | tf_op jit(solution)/shard_map/dot_general | solution.py:58
  183.9 0.1 copy.21
  184.0 1.3 constant_dynamic-slice_fusion
  185.3 1.0 copy.28
  186.3 0.3 reshape.38
  186.6 2.9 copy.42
  189.5 96.2 %all-reduce.5.cloned.1.call-done = f32[4096,128]{0,1:T(8,128)} async-done(((f32[4096,128]{0,1:T(8,128)}), f32[4096,128]{0,1:T(8,128)}) %all-reduce.5.cloned.1.call-update) | async-done | bytes 2097168 | tf_op jit(solution)/shard_map/psum | solution.py:62
  285.7 3.3 fusion.26
  289.0 0.0 all-reduce.7.cloned.1.call-update
  289.1 2.7 multiply_reduce_fusion
  292.4 10.9 %psum.38 = f32[]{:T(128)} all-reduce(f32[]{:T(128)} %multiply_reduce_fusion), channel_id=1, replica_groups=mesh['dp'=32,'tensor'=4] {'tensor'}, use_global_device_ids=true, to_apply=%region_4.5 | all-reduce | flops 1 | bytes 8 | tf_op jit(solution)/shard_map/psum | solution.py:66
  303.9 26.1 %all-reduce.7.cloned.1.call-done = f32[128,128]{0,1:T(8,128)} async-done(((f32[128,128]{0,1:T(8,128)}), f32[128,128]{0,1:T(8,128)}) %all-reduce.7.cloned.1.call-update) | async-done | bytes 65552 | tf_op jit(solution)/shard_map/psum | solution.py:66
  330.0 0.8 multiply_add_fusion
  330.8 0.1 copy.22
  330.9 0.1 copy.23
  331.0 11.7 %cholesky.13 = f32[128,128]{1,0:T(8,128)S(1)} custom-call(f32[128,128]{1,0:T(8,128)S(1)} %fusion.14), custom_call_target="Cholesky" | custom-call | tf_op jit(solution)/shard_map/jit(cholesky)/cholesky | solution.py:71
  342.8 0.6 compare_reduce_fusion
  343.4 0.7 fusion.11
  344.1 9.8 %custom-call.7 = f32[1,128,128]{1,2,0:T(8,128)S(1)} custom-call(f32[1,128,128]{2,1,0:T(8,128)S(1)} %fusion.11), custom_call_target="InvertDiagBlocksLowerTriangular" | custom-call | tf_op jit(solution)/shard_map/jit(_solve_triangular)/triangular_solve | solution.py:73
  353.9 1.8 fusion.12
  (3 shorter events, 0.1 us)
Async XLA Ops:
  6.5 1.2 copy-start
  6.5 118.9 %all-gather.2.cloned.1.call-start = ((), (), s32[]{:S(2)}) async-start(), calls=%async_computation | async-start | bytes 30277632 | tf_op jit(solution)/shard_map/all_gather | solution.py:15
  7.3 278.4 %all-reduce.5.cloned.1.call-start = ((), (), s32[]{:S(2)}) async-start(), calls=%async_computation.1 | async-start | bytes 4194304 | tf_op jit(solution)/shard_map/psum | solution.py:62
  178.3 151.6 %all-reduce.7.cloned.1.call-start = ((), (), s32[]{:S(2)}) async-start(), calls=%async_computation.2 | async-start | bytes 131072 | tf_op jit(solution)/shard_map/psum | solution.py:66
Sparse Core Ops, SparseCore 0:
  9.5 115.8 all-gather.1
  178.4 107.2 all-reduce.4
  289.2 40.7 all-reduce.6
where the time goes:
time: 363 us; the launch traced here: 362 us
  waiting for transfers between devices  239 us (66%)
  matrix products  41.5 us (11%)
  blocking collectives  34 us (9%)
  other arithmetic  26.7 us (7%)
  between operations  14.4 us (4%)
  local copies, waits for them, and re-layouts  6.14 us (2%)
    all_gather x1, waiting for transfers between devices, local(): lax.all_gather(down_weight, 'dp', axis=1, tiled=True)  116 us
    psum x1, waiting for transfers between devices, local(): summed = lax.psum(sketch_part, 'dp')  96.2 us
    psum x1, waiting for transfers between devices, local(): lax.psum((jnp.sum(summed * summed), core_local), 'tensor')  26.1 us
    dot_general x1, matrix products, local(): lax.dot_general(gate_grad, out_proj, (((1,), (1,)), ((), ())), preferred_...  24.7 us
    psum x1, blocking collectives, local(): act_sum, out_sum = lax.psum((act_part, out_part), 'tensor')  23.1 us
    another operation x3, other arithmetic, local(): lower = jnp.linalg.cholesky(core)  12.4 us
    psum x1, blocking collectives, local(): lax.psum((jnp.sum(summed * summed), core_local), 'tensor')  10.9 us
    another operation x2, other arithmetic, local(): factor = jax.scipy.linalg.solve_triangular(lower, shifted.T, lower=True).T  10.5 us
  transfers between devices with their start and end apart: 3, of which 3 were waited for; matrix products, arithmetic and copies ran while one was open for 4% of the time, Pallas kernels for 0%

commit v1 on v0

--- a/solution.py
+++ b/solution.py
@@ -6,6 +6,15 @@
 SEQ_LEN = 128
 shift_scale = 0.1
 tiny_value = 1e-06
+
+
+def doubling_sum(array, name):
+    peers = lax.axis_size(name)
+    total, far = (array, 1)
+    while far < peers:
+        total = total + lax.ppermute(total, name, [(i, i ^ far) for i in range(peers)])
+        far = 2 * far
+    return total
 
 
 def local(tokens, grad_out, gate_pre, up_value, down_weight, in_proj, out_proj, test_matrix):
@@ -59,7 +68,7 @@
         test_matrix, test_matrix, (((0,), (0,)), ((), ())), preferred_element_type=jnp.float32
     )
     omega_sq = jnp.trace(gram)
-    summed = lax.psum(sketch_part, "dp")
+    summed = doubling_sum(sketch_part, "dp")
     core_local = lax.dot_general(
         omega_picked, summed, (((0,), (0,)), ((), ())), precision=lax.Precision.HIGHEST
     )

time: 363 us -> 448 us (1.23)
  waiting for transfers between devices: 239 us -> 319 us
  starting transfers between devices: 0.26 us -> 9.55 us
    ppermute x0 -> x5, waiting for transfers between devices: none -> 182 us  [doubling_sum(): lax.ppermute(total, name, [(i, i ^ far) for i in range(peers)])]
    psum x1 -> x0, waiting for transfers between devices: 96.2 us -> none  [local(): summed = lax.psum(sketch_part, 'dp')]
    ppermute x0 -> x5, starting transfers between devices: none -> 9.51 us  [doubling_sum(): lax.ppermute(total, name, [(i, i ^ far) for i in range(peers)])]
    psum x1, waiting for transfers between devices: 26.1 us -> 19.4 us  [local(): lax.psum((jnp.sum(summed * summed), core_local), 'tensor')]
  transfers between devices with their start and end apart: 3 -> 7, of which waited for: 3 -> 7; matrix products, arithmetic and copies ran while one was open for 4% -> 3% of each run, Pallas kernels for 0% -> 0%
where the time goes in v1:
time: 448 us
  waiting for transfers between devices  319 us (71%)
  matrix products  38.5 us (9%)
  blocking collectives  31.3 us (7%)
  other arithmetic  27.6 us (6%)
  between operations  14.9 us (3%)
  starting transfers between devices  9.55 us (2%)
  local copies, waits for them, and re-layouts  6.97 us (2%)
    ppermute x5, waiting for transfers between devices, doubling_sum(): lax.ppermute(total, name, [(i, i ^ far) for i in range(peers)])  182 us
    all_gather x1, waiting for transfers between devices, local(): lax.all_gather(down_weight, 'dp', axis=1, tiled=True)  116 us
    dot_general x1, matrix products, local(): lax.dot_general(gate_grad, out_proj, (((1,), (1,)), ((), ())), preferred_...  24.7 us
    psum x1, blocking collectives, local(): act_sum, out_sum = lax.psum((act_part, out_part), 'tensor')  23.1 us
    psum x1, waiting for transfers between devices, local(): lax.psum((jnp.sum(summed * summed), core_local), 'tensor')  19.4 us
    another operation x3, other arithmetic, local(): lower = jnp.linalg.cholesky(core)  12.4 us
    another operation x2, other arithmetic, local(): factor = jax.scipy.linalg.solve_triangular(lower, shifted.T, lower=True).T  10.5 us
    ppermute x5, starting transfers between devices, doubling_sum(): lax.ppermute(total, name, [(i, i ^ far) for i in range(peers)])  9.51 us
  transfers between devices with their start and end apart: 7, of which 7 were waited for; matrix products, arithmetic and copies ran while one was open for 3% of the time, Pallas kernels for 0%

profile of v1, /device:TPU:0, one launch (start us, length us, event | category | flops | bytes accessed | tf_op | source)
XLA Modules:
  0.0 447.6 jit_solution(15350555425189564253)
XLA Ops:
  6.5 0.0 copy-start
  6.5 0.0 all-gather.2.cloned.1.call-start
  6.5 0.7 all-gather.2.cloned.1.call-update
  7.3 0.0 all-reduce.4.cloned.1.call-start
  7.3 0.5 copy-done
  7.8 1.4 fusion.24
  9.1 116.3 %all-gather.2.cloned.1.call-done = bf16[3584,4096]{1,0:T(8,128)(2,1)} async-done(((bf16[3584,128]{1,0:T(8,128)(2,1)}), bf16[3584,4096]{1,0:T(8,128)(2,1)}) %all-gather.2.cloned.1.call-update) | async-done | bytes 29360144 | tf_op jit(solution)/shard_map/all_gather | solution.py:24
  125.4 24.7 %fusion.25 = f32[512,128]{1,0:T(8,128)S(1)} fusion(bf16[128,3584]{1,0:T(8,128)(2,1)} %param.14, bf16[512,3584]{1,0:T(8,128)(2,1)} %param.10, bf16[512,3584]{1,0:T(8,128)(2,1)} %param.11, bf16[512,4096]{1,0:T(8,128)(2,1)} %param.9, bf16[3584,4096]{1,0:T(8,128)(2,1)} %all-gather.2.cloned.1.call-done), kind=kOutput, calls=%fused_computation.40 | convolution fusion | flops 15524167680 | bytes 42074112 | tf_op jit(solution)/shard_map/dot_general | solution.py:36
  150.1 23.1 %all-reduce.5 = (bf16[512,128]{1,0:T(8,128)(2,1)S(1)}, bf16[512,128]{1,0:T(8,128)(2,1)S(1)}) all-reduce(f32[512,128]{1,0:T(8,128)S(1)} %fusion.24, f32[512,128]{1,0:T(8,128)S(1)} %fusion.25), channel_id=1, replica_groups=mesh['dp'=32,'tensor'=4] {'tensor'}, use_global_device_ids=true, to_apply=%region_0.0 | all-reduce | flops 131072 | bytes 786432 | tf_op jit(solution)/shard_map/psum | solution.py:39
  173.2 0.2 convolution_convert_fusion
  173.4 0.2 dynamic-slice_reduce_fusion
  173.7 3.3 fusion.6
  177.0 0.1 collective-permute-start
  177.1 4.1 collective-permute-done
  181.2 0.3 add.64
  181.5 1.6 collective-permute-start.1
  183.1 46.1 %collective-permute-done.1 = f32[4096,128]{0,1:T(8,128)S(1)} collective-permute-done((f32[4096,128]{0,1:T(8,128)S(1)}, f32[4096,128]{0,1:T(8,128)S(1)}, u32[]{:S(2)}, u32[]{:S(2)}) %collective-permute-start.1) | collective-permute-done | bytes 2097184 | tf_op jit(solution)/shard_map/ppermute | solution.py:15
  229.2 0.3 add.65
  229.5 2.9 collective-permute-start.2
  232.4 45.5 %collective-permute-done.2 = f32[4096,128]{0,1:T(8,128)S(1)} collective-permute-done((f32[4096,128]{0,1:T(8,128)S(1)}, f32[4096,128]{0,1:T(8,128)S(1)}, u32[]{:S(2)}, u32[]{:S(2)}) %collective-permute-start.2) | collective-permute-done | bytes 2097184 | tf_op jit(solution)/shard_map/ppermute | solution.py:15
  277.9 0.3 add.66
  278.2 1.6 collective-permute-start.3
  279.8 44.5 %collective-permute-done.3 = f32[4096,128]{0,1:T(8,128)S(1)} collective-permute-done((f32[4096,128]{0,1:T(8,128)S(1)}, f32[4096,128]{0,1:T(8,128)S(1)}, u32[]{:S(2)}, u32[]{:S(2)}) %collective-permute-start.3) | collective-permute-done | bytes 2097184 | tf_op jit(solution)/shard_map/ppermute | solution.py:15
  324.2 0.3 add.67
  324.5 3.3 collective-permute-start.4
  327.8 1.3 constant_dynamic-slice_fusion
  329.1 42.2 %collective-permute-done.4 = f32[4096,128]{0,1:T(8,128)S(1)} collective-permute-done((f32[4096,128]{0,1:T(8,128)S(1)}, f32[4096,128]{0,1:T(8,128)S(1)}, u32[]{:S(2)}, u32[]{:S(2)}) %collective-permute-start.4) | collective-permute-done | bytes 2097184 | tf_op jit(solution)/shard_map/ppermute | solution.py:15
  371.3 1.2 multiply_reduce_fusion
  372.6 1.8 fusion.26
  374.3 0.0 all-reduce.4.cloned.1.call-update
  374.3 5.4 %select_reduce_fusion.1 = (f32[]{:T(128)}, f32[128,128]{1,0:T(8,128)S(1)}) fusion(bf16[16384,128]{1,0:T(8,128)(2,1)} %param.15), kind=kOutput, calls=%fused_computation.29 | convolution fusion | flops 536920064 | bytes 4259844 | tf_op jit(solution)/shard_map/dot_general | solution.py:67
  379.7 1.7 copy.30
  381.5 0.0 copy-start.1
  381.5 0.1 copy.23
  381.6 1.6 reshape.38
  383.1 3.0 copy.44
  386.8 8.3 %psum.30 = f32[]{:T(128)} all-reduce(f32[]{:T(128)} %get-tuple-element.7), channel_id=1, replica_groups=mesh['dp'=32,'tensor'=4] {'tensor'}, use_global_device_ids=true, to_apply=%region_3.4 | all-reduce | flops 1 | bytes 8 | tf_op jit(solution)/shard_map/psum | solution.py:75
  395.7 19.4 %all-reduce.4.cloned.1.call-done = f32[128,128]{0,1:T(8,128)} async-done(((f32[128,128]{0,1:T(8,128)}), f32[128,128]{0,1:T(8,128)}) %all-reduce.4.cloned.1.call-update) | async-done | bytes 65552 | tf_op jit(solution)/shard_map/psum | solution.py:75
  415.1 0.8 multiply_add_fusion
  415.9 0.1 copy.24
  416.0 0.1 copy.25
  416.2 11.7 %cholesky.13 = f32[128,128]{1,0:T(8,128)S(1)} custom-call(f32[128,128]{1,0:T(8,128)S(1)} %fusion.14), custom_call_target="Cholesky" | custom-call | tf_op jit(solution)/shard_map/jit(cholesky)/cholesky | solution.py:80
  427.9 0.6 compare_reduce_fusion
  428.5 0.7 fusion.11
  429.2 9.8 %custom-call.7 = f32[1,128,128]{1,2,0:T(8,128)S(1)} custom-call(f32[1,128,128]{2,1,0:T(8,128)S(1)} %fusion.11), custom_call_target="InvertDiagBlocksLowerTriangular" | custom-call | tf_op jit(solution)/shard_map/jit(_solve_triangular)/triangular_solve | solution.py:82
  439.0 1.8 fusion.12
  440.8 0.0 copy-done.1
  (3 shorter events, 0.1 us)
Async XLA Ops:
  6.5 1.2 copy-start
  6.5 118.9 %all-gather.2.cloned.1.call-start = ((), (), s32[]{:S(2)}) async-start(), calls=%async_computation | async-start | bytes 30277632 | tf_op jit(solution)/shard_map/all_gather | solution.py:24
  7.3 407.8 %all-reduce.4.cloned.1.call-start = ((), (), s32[]{:S(2)}) async-start(), calls=%async_computation.1 | async-start | bytes 131072 | tf_op jit(solution)/shard_map/psum | solution.py:75
  177.0 4.2 collective-permute-start
  181.5 47.8 %collective-permute-start.1 = (f32[4096,128]{0,1:T(8,128)S(1)}, f32[4096,128]{0,1:T(8,128)S(1)}, u32[]{:S(2)}, u32[]{:S(2)}) collective-permute-start(f32[4096,128]{0,1:T(8,128)S(1)} %add.64), channel_id=1, source_target_pairs={{0,8},{4,12},{8,0},{12,4},{16,24},{20,28},{24,16},{28,20},{32,40},... | collective-permute-start | bytes 6291464 | tf_op jit(solution)/shard_map/ppermute | solution.py:15
  229.5 48.4 %collective-permute-start.2 = (f32[4096,128]{0,1:T(8,128)S(1)}, f32[4096,128]{0,1:T(8,128)S(1)}, u32[]{:S(2)}, u32[]{:S(2)}) collective-permute-start(f32[4096,128]{0,1:T(8,128)S(1)} %add.65), channel_id=1, source_target_pairs={{0,16},{4,20},{8,24},{12,28},{16,0},{20,4},{24,8},{28,12},{32,48},... | collective-permute-start | bytes 6291464 | tf_op jit(solution)/shard_map/ppermute | solution.py:15
  278.2 46.0 %collective-permute-start.3 = (f32[4096,128]{0,1:T(8,128)S(1)}, f32[4096,128]{0,1:T(8,128)S(1)}, u32[]{:S(2)}, u32[]{:S(2)}) collective-permute-start(f32[4096,128]{0,1:T(8,128)S(1)} %add.66), channel_id=1, source_target_pairs={{0,32},{4,36},{8,40},{12,44},{16,48},{20,52},{24,56},{28,60},{32,0... | collective-permute-start | bytes 6291464 | tf_op jit(solution)/shard_map/ppermute | solution.py:15
  324.5 46.9 %collective-permute-start.4 = (f32[4096,128]{0,1:T(8,128)S(1)}, f32[4096,128]{0,1:T(8,128)S(1)}, u32[]{:S(2)}, u32[]{:S(2)}) collective-permute-start(f32[4096,128]{0,1:T(8,128)S(1)} %add.67), channel_id=1, source_target_pairs={{0,64},{4,68},{8,72},{12,76},{16,80},{20,84},{24,88},{28,92},{32,9... | collective-permute-start | bytes 6291464 | tf_op jit(solution)/shard_map/ppermute | solution.py:15
  381.5 59.3 %copy-start.1 = (bf16[512,1024]{1,0:T(8,128)(2,1)S(1)}, bf16[512,1024]{1,0:T(8,128)(2,1)}, u32[]{:S(2)}) copy-start(bf16[512,1024]{1,0:T(8,128)(2,1)} %param.8) | copy-start | bytes 3145732
Sparse Core Ops, SparseCore 0:
  9.5 115.8 all-gather.1
  374.5 40.5 all-reduce.3
